TPU v7x, 128 devices: a whole 4x4x4 slice. The times are simulated.
128 devices in a mesh: feat: 8 (over x_lo, y), dp: 16 (over z, x_hi, core).
Axes of the slice: x: 4 (x_hi: 2, x_lo: 2; x = x_hi * 2 + x_lo), y: 4, z: 4, core: 2. Of those that a mesh axis runs over, the one named last changes fastest.
Arguments:
- text_rows: bfloat16 [2048, 8192], P('dp', 'feat'), may hold values from -6 to 6
- q_weight: bfloat16 [8192, 8192], P(None, 'feat'), may hold values from -0.0625 to 0.0625
- features: bfloat16 [16, 1024, 7680], P('dp', None, 'feat'), may hold values from -6 to 6
- kv_weight: bfloat16 [7680, 2048], P('feat'), may hold values from -0.0625 to 0.0625
- q_gain: float32 [128], replicated, may hold values from 0.7 to 2.6
- k_gain: float32 [128], replicated, may hold values from 0.7 to 2.6
- attn_gate: float32 [1], replicated, may hold values from 0.5 to 2
- image_ids: int32 [256, 2], P('dp'), may hold values from 0 to 15, all different within a row; in each aligned block of 16 rows (0 to 15, 16 to 31, ...) at most 4 rows name the same one
- image_slot: int32 [16], replicated, may hold values from 0 to 15, each once
Outputs:
- attended: bfloat16 [2048, 8192], P('dp', 'feat')
Inputs may be any that keep to these rules, and one draw needn't show every extreme that they name: `image_ids`: each request names two different images; among the requests of one index of dp (aligned blocks of 16 requests) no image is named more than 4 times, a bound that some block reaches. Each position once; image i lies at position image_slot[i].
All inputs are finite; a program needn't handle non-finite values.
Results may differ from a plain program's by a relative error of at most 0.009.
The roundings to bfloat16 on the way count: a program that leaves them out, or rounds other values in their place, can miss the bound.
Values may be sent and summed in bfloat16 or wider, within the bound.
No kernel may reach another device: no remote copies, remote signals or barrier semaphores. Data moves between devices by JAX's collectives and lax.ppermute only.
A program may use at most 128 MiB of HBM per device.

v0:
```python
import jax
import jax.numpy as jnp
from jax import lax
from jax.sharding import PartitionSpec as P

epsilon = 1e-05


def head_norm(values, gain_vector):
    return (
        values
        * lax.rsqrt(jnp.mean(values * values, axis=-1, keepdims=True) + epsilon)
        * gain_vector
    )


def attend(queries, keyval, weights):
    head_width = queries.shape[-1]
    scores = jnp.einsum(
        "rhgd,hnd->rhgn", queries, keyval[..., :head_width], preferred_element_type=jnp.float32
    )
    exponent = jnp.exp(scores)
    exponent = exponent * weights[:, None, None, None]
    exponent = exponent.astype(jnp.bfloat16)
    denominator = jnp.sum(exponent.astype(jnp.float32), axis=-1)
    numerator = jnp.einsum(
        "rhgn,hnd->rhgd", exponent, keyval[..., head_width:], preferred_element_type=jnp.float32
    )
    return (numerator, denominator)


def per_device(
    text_rows, q_weight, features, kv_weight, q_gain, k_gain, attn_gate, image_ids, image_slot
):
    row_count = text_rows.shape[0]
    requests = image_ids.shape[0]
    text_words = row_count // requests
    head_width = q_gain.shape[0]
    heads_all = kv_weight.shape[1] // (2 * head_width)
    kv_local = heads_all // lax.axis_size("feat")
    group_size = q_weight.shape[1] // (head_width * kv_local)
    weight_block = q_weight
    queries = jnp.dot(
        lax.all_gather(text_rows, "feat", axis=1, tiled=True),
        weight_block,
        preferred_element_type=jnp.float32,
    )
    queries = head_norm(
        queries.reshape(row_count, kv_local, group_size, head_width), q_gain
    ) * head_width ** (-0.5)
    queries = queries.astype(jnp.bfloat16)
    kv_table = kv_weight.reshape(kv_weight.shape[0], heads_all, 2 * head_width)
    vision_rows = features[0]
    weight_block = kv_table
    summed = lax.psum_scatter(
        jnp.einsum("nf,fhc->hnc", vision_rows, weight_block, preferred_element_type=jnp.float32),
        "feat",
        scatter_dimension=0,
        tiled=True,
    )
    normed_keys = head_norm(summed[..., :head_width], k_gain)
    keyval = jnp.concatenate([normed_keys, summed[..., head_width:]], axis=-1).astype(jnp.bfloat16)
    image_count = image_slot.shape[0]
    matches = image_ids[:, :, None] == jnp.arange(image_count, dtype=jnp.int32)[None, None, :]
    owners = jnp.sum(jnp.where(matches, image_slot[None, None, :], 0), axis=-1)
    starting = (
        jnp.zeros((row_count, kv_local, group_size, head_width), jnp.float32),
        jnp.zeros((row_count, kv_local, group_size), jnp.float32),
    )
    shard_piece = lax.all_gather(keyval[None], "dp", axis=0, tiled=True)

    def add_one(position, partial_sums):
        reads_image = jnp.any(owners == position, axis=1)
        weights = jnp.repeat(reads_image.astype(jnp.float32), text_words)
        kv_block = lax.dynamic_index_in_dim(shard_piece, position, 0, keepdims=False)
        numerator, denominator = attend(queries, kv_block, weights)
        return (partial_sums[0] + numerator, partial_sums[1] + denominator)

    numerator, denominator = lax.fori_loop(0, shard_piece.shape[0], add_one, starting)
    result = numerator / denominator[..., None]
    return (jnp.tanh(attn_gate[0]) * result).astype(jnp.bfloat16).reshape(row_count, -1)


def solution(mesh):
    in_specs = (
        P("dp", "feat"),
        P(None, "feat"),
        P("dp", None, "feat"),
        P("feat", None),
        P(),
        P(),
        P(),
        P("dp", None),
        P(),
    )
    out_specs = P("dp", "feat")
    return jax.shard_map(
        per_device, mesh=mesh, in_specs=in_specs, out_specs=out_specs, check_vma=False
    )
```

profile of v0, /device:TPU:1, one launch (start us, length us, event | category | flops | bytes accessed | tf_op | source)
XLA Modules:
  0.0 329.7 jit_solution(1036196203318548550)
XLA Ops:
  6.5 1.5 copy-done
  8.1 9.0 %fusion.13 = f32[8,1024,256]{1,2,0:T(8,128)} fusion(bf16[120,8,8,256]{3,2,1,0:T(8,128)(2,1)} %bitcast.86, bf16[1,1024,960]{1,2,0:T(8,128)(2,1)S(1)} %copy-done), kind=kOutput, calls=%fused_computation.16 | convolution fusion | flops 4026531840 | bytes 14286848 | tf_op jit(solution)/shard_map/nf,fhc->hnc/dot_general | solution.py:56
  17.2 0.7 all-gather.5.cloned.1.call-update
  17.9 95.3 %reduce-scatter.2.cloned.1.call-done = f32[1,1024,256]{1,2,0:T(8,128)} async-done(((f32[8,1024,256]{1,2,0:T(8,128)}), f32[1,1024,256]{1,2,0:T(8,128)}) %reduce-scatter.2.cloned.1.call-update) | async-done | bytes 1048592 | tf_op jit(solution)/shard_map/reduce_scatter | solution.py:55
  113.2 1.1 multiply_reduce_fusion.1
  114.3 1.1 fusion.21
  115.4 1.1 fusion.20
  116.6 1.0 copy.42
  118.4 0.2 select_reduce_fusion
  118.5 31.4 %all-gather.5.cloned.1.call-done = bf16[128,8192]{1,0:T(8,128)(2,1)} async-done(((bf16[128,1024]{1,0:T(8,128)(2,1)}), bf16[128,8192]{1,0:T(8,128)(2,1)}) %all-gather.5.cloned.1.call-update) | async-done | bytes 2097168 | tf_op jit(solution)/shard_map/all_gather | solution.py:44
  149.9 8.7 %convolution_bitcast_fusion = f32[16,8,8,128]{3,1,2,0:T(8,128)S(1)} fusion(bf16[128,8192]{1,0:T(8,128)(2,1)} %all-gather.5.cloned.1.call-done, bf16[8192,1024]{1,0:T(8,128)(2,1)} %param.12), kind=kOutput, calls=%fused_computation.18 | convolution fusion | flops 2147483648 | bytes 19398656 | tf_op jit(solution)/shard_map/dot_general | solution.py:43
  158.7 0.2 multiply_reduce_fusion
  159.0 0.2 fusion.19
  159.3 71.2 %all-gather.3.cloned.1.call-done = bf16[16,1,1024,256]{3,2,1,0:T(8,128)(2,1)} async-done(((bf16[1,1,1024,256]{3,2,1,0:T(8,128)(2,1)}), bf16[16,1,1024,256]{3,2,1,0:T(8,128)(2,1)}) %all-gather.3.cloned.1.call-update) | async-done | bytes 8388624 | tf_op jit(solution)/shard_map/all_gather | solution.py:70
  230.5 91.7 %while.16 = (s32[]{:T(128)}, f32[128,1,8,128]{0,3,2,1:T(8,128)S(1)}, f32[128,1,8]{0,2,1:T(8,128)S(1)}, bf16[16,1,1024,256]{3,2,1,0:T(8,128)(2,1)}, bf16[128,1,8,...) while((s32[]{:T(128)}, f32[128,1,8,128]{0,3,2,1:T(8,128)S(1)}, ...), condition=%wide.region_7.8_spmd.clone, body=%wide.region_4.7_spmd.clone.sunk | while | flops 541328448 | bytes 7096712 | solution.py:79
  230.5 1.1 dynamic-slice_bitcast_fusion.2
  231.8 2.3 convert_reduce_fusion.2
  234.1 2.1 fusion.27
  236.2 1.1 dynamic-slice_bitcast_fusion.2
  237.5 2.3 convert_reduce_fusion.2
  239.8 2.1 fusion.27
  242.0 1.1 dynamic-slice_bitcast_fusion.2
  243.2 2.3 convert_reduce_fusion.2
  245.5 2.1 fusion.27
  247.7 1.1 dynamic-slice_bitcast_fusion.2
  249.0 2.3 convert_reduce_fusion.2
  251.3 2.1 fusion.27
  253.4 1.1 dynamic-slice_bitcast_fusion.2
  254.7 2.3 convert_reduce_fusion.2
  257.0 2.1 fusion.27
  259.2 1.1 dynamic-slice_bitcast_fusion.2
  260.4 2.3 convert_reduce_fusion.2
  262.7 2.1 fusion.27
  264.9 1.1 dynamic-slice_bitcast_fusion.2
  266.2 2.3 convert_reduce_fusion.2
  268.5 2.1 fusion.27
  270.6 1.1 dynamic-slice_bitcast_fusion.2
  271.9 2.3 convert_reduce_fusion.2
  274.2 2.1 fusion.27
  276.4 1.1 dynamic-slice_bitcast_fusion.2
  277.6 2.3 convert_reduce_fusion.2
  279.9 2.1 fusion.27
  282.1 1.1 dynamic-slice_bitcast_fusion.2
  283.4 2.3 convert_reduce_fusion.2
  285.7 2.1 fusion.27
  287.8 1.1 dynamic-slice_bitcast_fusion.2
  289.1 2.3 convert_reduce_fusion.2
  291.4 2.1 fusion.27
  293.6 1.1 dynamic-slice_bitcast_fusion.2
  294.9 2.3 convert_reduce_fusion.2
  297.1 2.1 fusion.27
  299.3 1.1 dynamic-slice_bitcast_fusion.2
  300.6 2.3 convert_reduce_fusion.2
  302.9 2.1 fusion.27
  305.0 1.1 dynamic-slice_bitcast_fusion.2
  306.3 2.3 convert_reduce_fusion.2
  308.6 2.1 fusion.27
  310.8 1.1 dynamic-slice_bitcast_fusion.2
  312.1 2.3 convert_reduce_fusion.2
  314.3 2.1 fusion.27
  316.5 1.1 dynamic-slice_bitcast_fusion.2
  317.8 2.3 convert_reduce_fusion.2
  320.1 2.1 fusion.27
  322.3 0.9 copy.48
  (102 shorter events, 3.6 us)
Async XLA Ops:
  6.5 1.5 copy-start
  6.5 106.6 %reduce-scatter.2.cloned.1.call-start = ((), (), s32[]{:S(2)}) async-start(), calls=%async_computation.1 | async-start | bytes 9437184 | tf_op jit(solution)/shard_map/reduce_scatter | solution.py:55
  17.1 98.3 %copy-start.3 = (f32[128]{0:T(128)S(1)}, f32[128]{0:T(128)}, u32[]{:S(2)}) copy-start(f32[128]{0:T(128)} %param.16) | copy-start | bytes 1540
  17.1 101.2 %copy-start.1 = (s32[16,2]{0,1:T(2,128)S(1)}, s32[16,2]{0,1:T(2,128)}, u32[]{:S(2)}) copy-start(s32[16,2]{0,1:T(2,128)} %param.18) | copy-start | bytes 388
  17.1 101.2 %copy-start.2 = (s32[16]{0:T(128)S(1)}, s32[16]{0:T(128)}, u32[]{:S(2)}) copy-start(s32[16]{0:T(128)} %param.19) | copy-start | bytes 196
  17.1 132.8 %all-gather.5.cloned.1.call-start = ((), (), s32[]{:S(2)}) async-start(), calls=%async_computation.3 | async-start | bytes 2359296 | tf_op jit(solution)/shard_map/all_gather | solution.py:44
  17.9 212.6 %all-gather.3.cloned.1.call-start = ((), (), s32[]{:S(2)}) async-start(), calls=%async_computation.2 | async-start | bytes 8912896 | tf_op jit(solution)/shard_map/all_gather | solution.py:70
  118.5 40.5 %copy-start.4 = (f32[128]{0:T(128)S(1)}, f32[128]{0:T(128)}, u32[]{:S(2)}) copy-start(f32[128]{0:T(128)} %param.15) | copy-start | bytes 1540
Sparse Core Ops, SparseCore 0:
  17.2 95.9 reduce-scatter.1
  114.8 35.0 all-gather.4
  152.4 78.0 all-gather.2
where the time goes:
time: 331 us; the launch traced here: 330 us
  waiting for transfers between devices  199 us (60%)
  matrix products  88.4 us (27%)
  local copies, waits for them, and re-layouts  24.5 us (7%)
  between operations  13.9 us (4%)
  other arithmetic  3.55 us (1%)
    reduce_scatter x1, waiting for transfers between devices, per_device(): lax.psum_scatter(jnp.einsum('nf,fhc->hnc', vision_rows, weight_block, pre...  95.3 us
    all_gather x1, waiting for transfers between devices, per_device(): shard_piece = lax.all_gather(keyval[None], 'dp', axis=0, tiled=True)  71.2 us
    dot_general x16, matrix products, attend(): jnp.einsum('rhgd,hnd->rhgn', queries, keyval[..., :head_width], preferred...  36.6 us
    dot_general x16, matrix products, attend(): jnp.einsum('rhgn,hnd->rhgd', exponent, keyval[..., head_width:], preferre...  34.2 us
    all_gather x1, waiting for transfers between devices, per_device(): lax.all_gather(text_rows, 'feat', axis=1, tiled=True)  31.4 us
    squeeze x16, local copies, waits for them, and re-layouts, add_one(): lax.dynamic_index_in_dim(shard_piece, position, 0, keepdims=False)  17.3 us
    dot_general x1, matrix products, per_device(): jnp.einsum('nf,fhc->hnc', vision_rows, weight_block, preferred_element_ty...  8.98 us
    dot_general x1, matrix products, per_device(): jnp.dot(lax.all_gather(text_rows, 'feat', axis=1, tiled=True), weight_blo...  8.74 us
  transfers between devices with their start and end apart: 3, of which 3 were waited for; matrix products, arithmetic and copies ran while one was open for 4% of the time, Pallas kernels for 0%

commit v1 on v0

--- a/solution.py
+++ b/solution.py
@@ -67,7 +67,9 @@
         jnp.zeros((row_count, kv_local, group_size, head_width), jnp.float32),
         jnp.zeros((row_count, kv_local, group_size), jnp.float32),
     )
-    shard_piece = lax.all_gather(keyval[None], "dp", axis=0, tiled=True)
+    shard_piece = jnp.concatenate(
+        lax.all_to_all(jnp.stack([keyval[None]] * lax.axis_size("dp")), "dp", 0, 0), axis=0
+    )
 
     def add_one(position, partial_sums):
         reads_image = jnp.any(owners == position, axis=1)

time: 331 us -> 345 us (1.042)
  starting transfers between devices: 0.08 us -> 7.37 us
    all_gather x1 -> x0, waiting for transfers between devices: 71.2 us -> none  [per_device(): shard_piece = lax.all_gather(keyval[None], 'dp', axis=0, tiled=True)]
    all_to_all x0 -> x1, waiting for transfers between devices: none -> 52.3 us  [per_device(): lax.all_to_all(jnp.stack([keyval[None]] * lax.axis_size('dp')), 'dp', 0, 0)]
    all_gather x1, waiting for transfers between devices: 31.4 us -> 52.6 us  [per_device(): lax.all_gather(text_rows, 'feat', axis=1, tiled=True)]
    all_to_all x0 -> x1, starting transfers between devices: none -> 7.33 us  [per_device(): lax.all_to_all(jnp.stack([keyval[None]] * lax.axis_size('dp')), 'dp', 0, 0)]
    another operation x0 -> x1, local copies, waits for them, and re-layouts: none -> 4.02 us  [per_device(): jnp.stack([keyval[None]] * lax.axis_size('dp'))]
  transfers between devices with their start and end apart: 3 -> 3, of which waited for: 3 -> 3; matrix products, arithmetic and copies ran while one was open for 4% -> 3% of each run, Pallas kernels for 0% -> 0%
where the time goes in v1:
time: 345 us; the launch traced here: 344 us
  waiting for transfers between devices  202 us (59%)
  matrix products  88.4 us (26%)
  local copies, waits for them, and re-layouts  27.7 us (8%)
  between operations  14.2 us (4%)
  starting transfers between devices  7.37 us (2%)
  other arithmetic  3.55 us (1%)
    reduce_scatter x1, waiting for transfers between devices, per_device(): lax.psum_scatter(jnp.einsum('nf,fhc->hnc', vision_rows, weight_block, pre...  96.1 us
    all_gather x1, waiting for transfers between devices, per_device(): lax.all_gather(text_rows, 'feat', axis=1, tiled=True)  52.6 us
    all_to_all x1, waiting for transfers between devices, per_device(): lax.all_to_all(jnp.stack([keyval[None]] * lax.axis_size('dp')), 'dp', 0, 0)  52.3 us
    dot_general x16, matrix products, attend(): jnp.einsum('rhgd,hnd->rhgn', queries, keyval[..., :head_width], preferred...  36.6 us
    dot_general x16, matrix products, attend(): jnp.einsum('rhgn,hnd->rhgd', exponent, keyval[..., head_width:], preferre...  34.2 us
    squeeze x16, local copies, waits for them, and re-layouts, add_one(): lax.dynamic_index_in_dim(shard_piece, position, 0, keepdims=False)  17.3 us
    dot_general x1, matrix products, per_device(): jnp.einsum('nf,fhc->hnc', vision_rows, weight_block, preferred_element_ty...  8.98 us
    dot_general x1, matrix products, per_device(): jnp.dot(lax.all_gather(text_rows, 'feat', axis=1, tiled=True), weight_blo...  8.74 us
  transfers between devices with their start and end apart: 3, of which 3 were waited for; matrix products, arithmetic and copies ran while one was open for 3% of the time, Pallas kernels for 0%

profile of v1, /device:TPU:1, one launch (start us, length us, event | category | flops | bytes accessed | tf_op | source)
XLA Modules:
  0.0 343.6 jit_solution(243336457351436233)
XLA Ops:
  6.5 1.5 copy-done
  8.1 9.0 %fusion.13 = f32[8,1024,256]{1,2,0:T(8,128)} fusion(bf16[120,8,8,256]{3,2,1,0:T(8,128)(2,1)} %bitcast.89, bf16[1,1024,960]{1,2,0:T(8,128)(2,1)S(1)} %copy-done), kind=kOutput, calls=%fused_computation.16 | convolution fusion | flops 4026531840 | bytes 14286848 | tf_op jit(solution)/shard_map/nf,fhc->hnc/dot_general | solution.py:56
  17.1 96.1 %reduce-scatter.2.cloned.1.call-done = f32[1,1024,256]{1,2,0:T(8,128)} async-done(((f32[8,1024,256]{1,2,0:T(8,128)}), f32[1,1024,256]{1,2,0:T(8,128)}) %reduce-scatter.2.cloned.1.call-update) | async-done | bytes 1048592 | tf_op jit(solution)/shard_map/reduce_scatter | solution.py:55
  113.2 1.1 multiply_reduce_fusion.1
  114.3 1.1 fusion.21
  115.4 1.1 fusion.20
  116.8 4.0 %stack.3 = bf16[16,1,1,1024,256]{4,3,2,1,0:T(8,128)(2,1)} broadcast(bf16[1024,256]{1,0:T(8,128)(2,1)S(1)} %copy.44), dimensions={3,4} | broadcast | bytes 8912896 | tf_op jit(solution)/shard_map/stack | solution.py:71
  120.8 7.3 %all-to-all-start = ((bf16[16,1,1,1024,256]{4,3,2,1,0:T(8,128)(2,1)}), bf16[16,1,1,1024,256]{4,3,2,1,0:T(8,128)(2,1)}, u32[]{:S(2)}, u32[]{:S(2)}) async-start(bf16[16,1,1,1024,256]{4,3,2,1,0:T(8,128)(2,1)} %stack.3), calls=%async_computation.1 | async-start | bytes 16777216 | tf_op jit(solution)/shard_map/all_to_all | solution.py:71
  128.2 0.7 all-gather.2.cloned.1.call-update
  129.8 52.6 %all-gather.2.cloned.1.call-done = bf16[128,8192]{1,0:T(8,128)(2,1)} async-done(((bf16[128,1024]{1,0:T(8,128)(2,1)}), bf16[128,8192]{1,0:T(8,128)(2,1)}) %all-gather.2.cloned.1.call-update) | async-done | bytes 2097168 | tf_op jit(solution)/shard_map/all_gather | solution.py:44
  182.4 8.7 %convolution_bitcast_fusion = f32[16,8,8,128]{3,1,2,0:T(8,128)S(1)} fusion(bf16[128,8192]{1,0:T(8,128)(2,1)} %all-gather.2.cloned.1.call-done, bf16[8192,1024]{1,0:T(8,128)(2,1)} %param.12), kind=kOutput, calls=%fused_computation.18 | convolution fusion | flops 2147483648 | bytes 19398656 | tf_op jit(solution)/shard_map/dot_general | solution.py:43
  191.2 0.2 multiply_reduce_fusion
  191.5 0.2 fusion.19
  191.7 52.3 %all-to-all-done = bf16[16,1,1,1024,256]{4,3,2,1,0:T(8,128)(2,1)} async-done(((bf16[16,1,1,1024,256]{4,3,2,1,0:T(8,128)(2,1)}), bf16[16,1,1,1024,256]{4,3,2,1,0:T(8,128)(2,1)}, u32[]{:S(2)}, u32[]{:S(2)}) %all-to-all-start) | async-done | bytes 8388640 | tf_op jit(solution)/shard_map/all_to_all | solution.py:71
  244.1 91.7 %while.16 = (s32[]{:T(128)}, f32[128,1,8,128]{0,3,2,1:T(8,128)S(1)}, f32[128,1,8]{0,2,1:T(8,128)S(1)}, bf16[16,1,1024,256]{3,2,1,0:T(8,128)(2,1)}, bf16[128,1,8,...) while((s32[]{:T(128)}, f32[128,1,8,128]{0,3,2,1:T(8,128)S(1)}, ...), condition=%wide.region_7.8_spmd.clone, body=%wide.region_4.7_spmd.clone.sunk | while | flops 541328448 | bytes 7096712 | solution.py:81
  244.1 1.1 dynamic-slice_bitcast_fusion.2
  245.4 2.3 convert_reduce_fusion.2
  247.6 2.1 fusion.27
  249.8 1.1 dynamic-slice_bitcast_fusion.2
  251.1 2.3 convert_reduce_fusion.2
  253.4 2.1 fusion.27
  255.5 1.1 dynamic-slice_bitcast_fusion.2
  256.8 2.3 convert_reduce_fusion.2
  259.1 2.1 fusion.27
  261.3 1.1 dynamic-slice_bitcast_fusion.2
  262.6 2.3 convert_reduce_fusion.2
  264.8 2.1 fusion.27
  267.0 1.1 dynamic-slice_bitcast_fusion.2
  268.3 2.3 convert_reduce_fusion.2
  270.6 2.1 fusion.27
  272.7 1.1 dynamic-slice_bitcast_fusion.2
  274.0 2.3 convert_reduce_fusion.2
  276.3 2.1 fusion.27
  278.5 1.1 dynamic-slice_bitcast_fusion.2
  279.8 2.3 convert_reduce_fusion.2
  282.0 2.1 fusion.27
  284.2 1.1 dynamic-slice_bitcast_fusion.2
  285.5 2.3 convert_reduce_fusion.2
  287.8 2.1 fusion.27
  290.0 1.1 dynamic-slice_bitcast_fusion.2
  291.2 2.3 convert_reduce_fusion.2
  293.5 2.1 fusion.27
  295.7 1.1 dynamic-slice_bitcast_fusion.2
  297.0 2.3 convert_reduce_fusion.2
  299.2 2.1 fusion.27
  301.4 1.1 dynamic-slice_bitcast_fusion.2
  302.7 2.3 convert_reduce_fusion.2
  305.0 2.1 fusion.27
  307.2 1.1 dynamic-slice_bitcast_fusion.2
  308.4 2.3 convert_reduce_fusion.2
  310.7 2.1 fusion.27
  312.9 1.1 dynamic-slice_bitcast_fusion.2
  314.2 2.3 convert_reduce_fusion.2
  316.5 2.1 fusion.27
  318.6 1.1 dynamic-slice_bitcast_fusion.2
  319.9 2.3 convert_reduce_fusion.2
  322.2 2.1 fusion.27
  324.4 1.1 dynamic-slice_bitcast_fusion.2
  325.6 2.3 convert_reduce_fusion.2
  327.9 2.1 fusion.27
  330.1 1.1 dynamic-slice_bitcast_fusion.2
  331.4 2.3 convert_reduce_fusion.2
  333.7 2.1 fusion.27
  335.9 0.9 copy.51
  (102 shorter events, 3.9 us)
Async XLA Ops:
  6.5 1.5 copy-start
  6.5 106.6 %reduce-scatter.2.cloned.1.call-start = ((), (), s32[]{:S(2)}) async-start(), calls=%async_computation.2 | async-start | bytes 9437184 | tf_op jit(solution)/shard_map/reduce_scatter | solution.py:55
  17.1 98.3 %copy-start.3 = (f32[128]{0:T(128)S(1)}, f32[128]{0:T(128)}, u32[]{:S(2)}) copy-start(f32[128]{0:T(128)} %param.16) | copy-start | bytes 1540
  120.8 8.8 %copy-start.1 = (s32[16,2]{0,1:T(2,128)S(1)}, s32[16,2]{0,1:T(2,128)}, u32[]{:S(2)}) copy-start(s32[16,2]{0,1:T(2,128)} %param.18) | copy-start | bytes 388
  120.8 8.8 %copy-start.2 = (s32[16]{0:T(128)S(1)}, s32[16]{0:T(128)}, u32[]{:S(2)}) copy-start(s32[16]{0:T(128)} %param.19) | copy-start | bytes 196
  120.8 123.3 %all-to-all-start = ((bf16[16,1,1,1024,256]{4,3,2,1,0:T(8,128)(2,1)}), bf16[16,1,1,1024,256]{4,3,2,1,0:T(8,128)(2,1)}, u32[]{:S(2)}, u32[]{:S(2)}) async-start(bf16[16,1,1,1024,256]{4,3,2,1,0:T(8,128)(2,1)} %stack.3), calls=%async_computation.1 | async-start | bytes 16777216 | tf_op jit(solution)/shard_map/all_to_all | solution.py:71
  128.1 54.2 %all-gather.2.cloned.1.call-start = ((), (), s32[]{:S(2)}) async-start(), calls=%async_computation.3 | async-start | bytes 2359296 | tf_op jit(solution)/shard_map/all_gather | solution.py:44
  129.8 61.7 %copy-start.4 = (f32[128]{0:T(128)S(1)}, f32[128]{0:T(128)}, u32[]{:S(2)}) copy-start(f32[128]{0:T(128)} %param.15) | copy-start | bytes 1540
Sparse Core Ops, SparseCore 0:
  17.2 95.9 reduce-scatter.1
  130.6 51.7 all-gather.1
